TPU v7x, 32 devices: a whole 2x2x4 slice. The times are simulated.
32 devices in a mesh: wide: 8 (over y, x, core), narrow: 4 (over z).
Axes of the slice: x: 2, y: 2, z: 4, core: 2. Of those that a mesh axis runs over, the one named last changes fastest.
Arguments:
- tokens: bfloat16 [4096, 4096], P(('wide', 'narrow')), may hold values from -6 to 6
- cotangent: bfloat16 [4096, 4096], P(('wide', 'narrow')), may hold values from -6 to 6
- weights: bfloat16 [32, 6, 256, 256], P(('wide', 'narrow')), may hold values from -0.1875 to 0.1875
- block_index: int32 [32, 6], P(('wide', 'narrow')), may hold values from 0 to 15, as said below
- block_counts: int32 [32], P(('wide', 'narrow')), may hold values from 1 to 6, as said below
Outputs:
- mixed: bfloat16 [4096, 4096], P(('wide', 'narrow'))
- grad_tokens: bfloat16 [4096, 4096], P(('wide', 'narrow'))
Inputs may be any that keep to these rules, and one draw needn't show every extreme that they name: `block_index`: each row lists 6 distinct blocks. `block_counts`: slots at or beyond a row's count are unused.
All inputs are finite; a program needn't handle non-finite values.
Results may differ from a plain program's by a relative error of at most 0.008.
Values may be sent and summed in bfloat16 or wider, within the bound.
No kernel may reach another device: no remote copies, remote signals or barrier semaphores. Data moves between devices by JAX's collectives and lax.ppermute only.
A program may use at most 192 MiB of HBM per device.

v0:
```python
import jax
import jax.numpy as jnp
from jax import lax
from jax.sharding import PartitionSpec as P


def from_root(block, axis, source):
    block = jnp.where(lax.axis_index(axis) == source, block, jnp.zeros_like(block))
    return lax.psum(block, axis)


def activate(values):
    return jax.nn.gelu(values, approximate=True)


def body(tokens, cotangent, weights, block_index, block_counts):
    rows_tok, rows_cot = (
        lax.all_gather(tokens, "narrow", axis=0, tiled=True),
        lax.all_gather(cotangent, "narrow", axis=0, tiled=True),
    )
    wide_count = lax.axis_size("wide")

    def receive(section_num, buffers):
        received = (
            from_root(weights, "wide", section_num),
            from_root(block_index, "wide", section_num),
            from_root(block_counts, "wide", section_num),
        )
        return tuple(
            (
                lax.dynamic_update_index_in_dim(buffer, piece[0], section_num, 0)
                for buffer, piece in zip(buffers, received)
            )
        )

    initial = (
        jnp.zeros((wide_count,) + weights.shape[1:], weights.dtype),
        jnp.zeros((wide_count, block_index.shape[1]), jnp.int32),
        jnp.zeros((wide_count,), jnp.int32),
    )
    blocks_all, indices_all, counts_all = lax.fori_loop(0, wide_count, receive, initial)
    half_wide = wide_count // 2
    num_slots = blocks_all.shape[1]
    block_width = blocks_all.shape[2]
    live_mask = (jnp.arange(num_slots)[None, :] < counts_all[:, None]).astype(jnp.bfloat16)
    kept_blocks = blocks_all * live_mask[:, :, None, None]
    num_rows = rows_tok.shape[0]
    num_blocks = rows_tok.shape[1] // block_width
    tok_blocks = rows_tok.reshape(num_rows, num_blocks, block_width)
    cot_blocks = rows_cot.reshape(num_rows, num_blocks, block_width)
    panel_items = (
        kept_blocks[:half_wide],
        indices_all[:half_wide],
        kept_blocks[half_wide:],
        indices_all[half_wide:],
    )
    zeros_acc = jnp.zeros((num_rows, num_blocks, block_width), jnp.float32)

    def forward(running, panel_item):
        w_first, idx_first, w_second, idx_second = panel_item
        picked = jnp.take(tok_blocks, idx_first, axis=1)
        pre_act = jnp.einsum("tjd,jdh->th", picked, w_first, preferred_element_type=jnp.float32)
        act_out = activate(pre_act).astype(jnp.bfloat16)
        running = running.at[:, idx_second].add(
            jnp.einsum("th,jhd->tjd", act_out, w_second, preferred_element_type=jnp.float32)
        )
        return (running, pre_act)

    def backward(running, panel_item):
        w_first, idx_first, w_second, idx_second, pre_act = panel_item
        cot_picked = jnp.take(cot_blocks, idx_second, axis=1)
        grad_act = jnp.einsum(
            "tjd,jhd->th", cot_picked, w_second, preferred_element_type=jnp.float32
        )
        grad_pre = jax.vjp(activate, pre_act)[1](grad_act)[0].astype(jnp.bfloat16)
        running = running.at[:, idx_first].add(
            jnp.einsum("th,jdh->tjd", grad_pre, w_first, preferred_element_type=jnp.float32)
        )
        return (running, None)

    out_acc, pre_stack = lax.scan(forward, zeros_acc, panel_items)
    grad_acc, _ = lax.scan(backward, zeros_acc, panel_items + (pre_stack,))
    out_part = out_acc.reshape(num_rows, -1).astype(jnp.bfloat16)
    grad_part = grad_acc.reshape(num_rows, -1).astype(jnp.bfloat16)
    mixed, grad_tokens = (
        lax.psum_scatter(out_part, "narrow", scatter_dimension=0, tiled=True).astype(jnp.float32),
        lax.psum_scatter(grad_part, "narrow", scatter_dimension=0, tiled=True).astype(jnp.float32),
    )
    return (mixed.astype(jnp.bfloat16), grad_tokens.astype(jnp.bfloat16))


def solution(mesh):
    placed = (
        P(("wide", "narrow"), None),
        P(("wide", "narrow"), None),
        P(("wide", "narrow"), None, None, None),
        P(("wide", "narrow"), None),
        P(("wide", "narrow")),
    )
    return jax.shard_map(
        body,
        mesh=mesh,
        in_specs=placed,
        out_specs=(P(("wide", "narrow"), None), P(("wide", "narrow"), None)),
        check_vma=False,
    )
```

profile of v0, /device:TPU:0, one launch (start us, length us, event | category | flops | bytes accessed | tf_op | source)
XLA Modules:
  0.0 832.8 jit_solution(13676505129722302704)
XLA Ops:
  10.3 494.1 %while.41 = (s32[]{:T(128)}, bf16[8,6,256,256]{3,2,1,0:T(8,128)(2,1)}, s32[8,6]{1,0:T(8,128)S(1)}, s32[8]{0:T(128)S(1)}, bf16[1,6,256,256]{3,2,1,0:T(8,128)(2,1)...) while((s32[]{:T(128)}, ...), condition=%wide.region_4.5_spmd, body=%wide.region_0.4_spmd.sunk | while | flops 786452 | bytes 7864713 | solution.py:41
  13.8 8.2 all-reduce.2
  22.7 50.4 %all-reduce.5.cloned.1.call-done = bf16[1,6,256,256]{3,2,1,0:T(8,128)(2,1)} async-done(((bf16[1,6,256,256]{3,2,1,0:T(8,128)(2,1)}), bf16[1,6,256,256]{3,2,1,0:T(8,128)(2,1)}) %all-reduce.5.cloned.1.call-update) | async-done | bytes 786448 | tf_op jit(solution)/shard_map/while/body/eval_jaxpr/psum | solution.py:9
  84.7 49.8 %all-reduce.5.cloned.1.call-done = bf16[1,6,256,256]{3,2,1,0:T(8,128)(2,1)} async-done(((bf16[1,6,256,256]{3,2,1,0:T(8,128)(2,1)}), bf16[1,6,256,256]{3,2,1,0:T(8,128)(2,1)}) %all-reduce.5.cloned.1.call-update) | async-done | bytes 786448 | tf_op jit(solution)/shard_map/while/body/eval_jaxpr/psum | solution.py:9
  138.3 7.8 all-reduce.2
  146.8 49.1 %all-reduce.5.cloned.1.call-done = bf16[1,6,256,256]{3,2,1,0:T(8,128)(2,1)} async-done(((bf16[1,6,256,256]{3,2,1,0:T(8,128)(2,1)}), bf16[1,6,256,256]{3,2,1,0:T(8,128)(2,1)}) %all-reduce.5.cloned.1.call-update) | async-done | bytes 786448 | tf_op jit(solution)/shard_map/while/body/eval_jaxpr/psum | solution.py:9
  207.6 49.5 %all-reduce.5.cloned.1.call-done = bf16[1,6,256,256]{3,2,1,0:T(8,128)(2,1)} async-done(((bf16[1,6,256,256]{3,2,1,0:T(8,128)(2,1)}), bf16[1,6,256,256]{3,2,1,0:T(8,128)(2,1)}) %all-reduce.5.cloned.1.call-update) | async-done | bytes 786448 | tf_op jit(solution)/shard_map/while/body/eval_jaxpr/psum | solution.py:9
  260.8 8.9 %all-reduce.2 = (s32[1,6]{1,0:T(1,128)S(1)}, s32[1]{0:T(128)}) all-reduce(s32[1,6]{1,0:T(1,128)S(1)} %broadcast_select_fusion.5, s32[1]{0:T(128)S(6)} %select_n.151), channel_id=1, replica_groups=mesh['wide'=8,'narrow'=4] {'wide'}, use_global_device_ids=true, to_apply=%region_2.2 | all-reduce | flops 7 | bytes 56 | tf_op jit(solution)/shard_map/while/body/eval_jaxpr/psum | solution.py:9
  270.5 47.7 %all-reduce.5.cloned.1.call-done = bf16[1,6,256,256]{3,2,1,0:T(8,128)(2,1)} async-done(((bf16[1,6,256,256]{3,2,1,0:T(8,128)(2,1)}), bf16[1,6,256,256]{3,2,1,0:T(8,128)(2,1)}) %all-reduce.5.cloned.1.call-update) | async-done | bytes 786448 | tf_op jit(solution)/shard_map/while/body/eval_jaxpr/psum | solution.py:9
  329.9 49.5 %all-reduce.5.cloned.1.call-done = bf16[1,6,256,256]{3,2,1,0:T(8,128)(2,1)} async-done(((bf16[1,6,256,256]{3,2,1,0:T(8,128)(2,1)}), bf16[1,6,256,256]{3,2,1,0:T(8,128)(2,1)}) %all-reduce.5.cloned.1.call-update) | async-done | bytes 786448 | tf_op jit(solution)/shard_map/while/body/eval_jaxpr/psum | solution.py:9
  383.1 8.5 %all-reduce.2 = (s32[1,6]{1,0:T(1,128)S(1)}, s32[1]{0:T(128)}) all-reduce(s32[1,6]{1,0:T(1,128)S(1)} %broadcast_select_fusion.5, s32[1]{0:T(128)S(6)} %select_n.151), channel_id=1, replica_groups=mesh['wide'=8,'narrow'=4] {'wide'}, use_global_device_ids=true, to_apply=%region_2.2 | all-reduce | flops 7 | bytes 56 | tf_op jit(solution)/shard_map/while/body/eval_jaxpr/psum | solution.py:9
  392.4 48.5 %all-reduce.5.cloned.1.call-done = bf16[1,6,256,256]{3,2,1,0:T(8,128)(2,1)} async-done(((bf16[1,6,256,256]{3,2,1,0:T(8,128)(2,1)}), bf16[1,6,256,256]{3,2,1,0:T(8,128)(2,1)}) %all-reduce.5.cloned.1.call-update) | async-done | bytes 786448 | tf_op jit(solution)/shard_map/while/body/eval_jaxpr/psum | solution.py:9
  452.4 49.8 %all-reduce.5.cloned.1.call-done = bf16[1,6,256,256]{3,2,1,0:T(8,128)(2,1)} async-done(((bf16[1,6,256,256]{3,2,1,0:T(8,128)(2,1)}), bf16[1,6,256,256]{3,2,1,0:T(8,128)(2,1)}) %all-reduce.5.cloned.1.call-update) | async-done | bytes 786448 | tf_op jit(solution)/shard_map/while/body/eval_jaxpr/psum | solution.py:9
  512.8 73.8 %all-gather.3.cloned.1.call-done = bf16[512,4096]{0,1:T(8,128)(2,1)} async-done(((bf16[128,4096]{0,1:T(8,128)(2,1)}), bf16[512,4096]{0,1:T(8,128)(2,1)}) %all-gather.3.cloned.1.call-update) | async-done | bytes 4194320 | tf_op jit(solution)/shard_map/all_gather | solution.py:18
  597.1 59.3 %while.42 = (s32[]{:T(128)}, f32[512,16,256]{2,0,1:T(8,128)}, f32[4,512,256]{2,1,0:T(8,128)}, s32[4,6]{1,0:T(4,128)S(1)}, s32[4,6]{1,0:T(4,128)S(1)}, /*index=5*...) while((s32[]{:T(128)}, f32[512,16,256]{2,0,1:T(8,128)}, ...), condition=%wide.region_7.9_spmd, body=%wide.region_5.8_spmd.sunk | while | flops 808059968 | bytes 20452644 | solution.py:81
  604.4 7.6 scatter_fusion
  619.2 7.6 scatter_fusion
  634.0 7.6 scatter_fusion
  648.8 7.6 scatter_fusion
  677.7 63.0 %while.43 = (s32[]{:T(128)}, f32[512,16,256]{2,0,1:T(8,128)}, s32[4,6]{1,0:T(4,128)S(1)}, s32[4,6]{1,0:T(4,128)S(1)}, bf16[512,16,256]{2,0,1:T(8,128)(2,1)}, /*i...) while((s32[]{:T(128)}, f32[512,16,256]{2,0,1:T(8,128)}, ...), condition=%wide.region_11.13_spmd, body=%wide.region_9.12_spmd.sunk | while | flops 809501760 | bytes 19404576 | solution.py:82
  685.8 7.6 scatter_fusion.1
  701.6 7.6 scatter_fusion.1
  717.4 7.6 scatter_fusion.1
  747.2 78.0 %reduce-scatter.5.cloned.1.call-done = bf16[128,4096]{1,0:T(8,128)(2,1)} async-done(((bf16[512,4096]{1,0:T(8,128)(2,1)}), bf16[128,4096]{1,0:T(8,128)(2,1)}) %reduce-scatter.5.cloned.1.call-update) | async-done | bytes 1048592 | tf_op jit(solution)/shard_map/reduce_scatter | solution.py:87
  (135 shorter events, 178.6 us)
Async XLA Ops:
  10.3 494.7 %copy-start = (bf16[128,4096]{1,0:T(8,128)(2,1)S(1)}, bf16[128,4096]{1,0:T(8,128)(2,1)}, u32[]{:S(2)}) copy-start(bf16[128,4096]{1,0:T(8,128)(2,1)} %param.14) | copy-start | bytes 3145732
  10.3 62.8 %all-reduce.5.cloned.1.call-start = ((), (), s32[]{:S(2)}) async-start(), calls=%async_computation.6 | async-start | bytes 1572864 | tf_op jit(solution)/shard_map/while/body/eval_jaxpr/psum | solution.py:9
  75.2 59.4 %all-reduce.5.cloned.1.call-start = ((), (), s32[]{:S(2)}) async-start(), calls=%async_computation.6 | async-start | bytes 1572864 | tf_op jit(solution)/shard_map/while/body/eval_jaxpr/psum | solution.py:9
  136.6 59.4 %all-reduce.5.cloned.1.call-start = ((), (), s32[]{:S(2)}) async-start(), calls=%async_computation.6 | async-start | bytes 1572864 | tf_op jit(solution)/shard_map/while/body/eval_jaxpr/psum | solution.py:9
  198.1 59.1 %all-reduce.5.cloned.1.call-start = ((), (), s32[]{:S(2)}) async-start(), calls=%async_computation.6 | async-start | bytes 1572864 | tf_op jit(solution)/shard_map/while/body/eval_jaxpr/psum | solution.py:9
  259.2 59.1 %all-reduce.5.cloned.1.call-start = ((), (), s32[]{:S(2)}) async-start(), calls=%async_computation.6 | async-start | bytes 1572864 | tf_op jit(solution)/shard_map/while/body/eval_jaxpr/psum | solution.py:9
  320.3 59.1 %all-reduce.5.cloned.1.call-start = ((), (), s32[]{:S(2)}) async-start(), calls=%async_computation.6 | async-start | bytes 1572864 | tf_op jit(solution)/shard_map/while/body/eval_jaxpr/psum | solution.py:9
  381.5 59.4 %all-reduce.5.cloned.1.call-start = ((), (), s32[]{:S(2)}) async-start(), calls=%async_computation.6 | async-start | bytes 1572864 | tf_op jit(solution)/shard_map/while/body/eval_jaxpr/psum | solution.py:9
  442.9 59.4 %all-reduce.5.cloned.1.call-start = ((), (), s32[]{:S(2)}) async-start(), calls=%async_computation.6 | async-start | bytes 1572864 | tf_op jit(solution)/shard_map/while/body/eval_jaxpr/psum | solution.py:9
  504.4 82.3 %all-gather.3.cloned.1.call-start = ((), (), s32[]{:S(2)}) async-start(), calls=%async_computation.2 | async-start | bytes 5242880 | tf_op jit(solution)/shard_map/all_gather | solution.py:18
  504.9 162.3 %all-gather.5.cloned.1.call-start = ((), (), s32[]{:S(2)}) async-start(), calls=%async_computation.4 | async-start | bytes 5242880 | tf_op jit(solution)/shard_map/all_gather | solution.py:19
  506.3 240.8 %reduce-scatter.3.cloned.1.call-start = ((), (), s32[]{:S(2)}) async-start(), calls=%async_computation.3 | async-start | bytes 5242880 | tf_op jit(solution)/shard_map/reduce_scatter | solution.py:86
  662.9 162.3 %reduce-scatter.5.cloned.1.call-start = ((), (), s32[]{:S(2)}) async-start(), calls=%async_computation.5 | async-start | bytes 5242880 | tf_op jit(solution)/shard_map/reduce_scatter | solution.py:87
Sparse Core Ops, SparseCore 0:
  14.8 58.2 all-reduce.4
  79.7 54.7 all-reduce.4
  141.2 54.7 all-reduce.4
  202.3 54.7 all-reduce.4
  263.4 54.7 all-reduce.4
  324.6 54.7 all-reduce.4
  386.0 54.7 all-reduce.4
  447.4 54.7 all-reduce.4
Sparse Core Ops, SparseCore 1:
  507.0 79.6 all-gather.2
  588.6 78.6 all-gather.4
  670.0 74.9 reduce-scatter.2
  748.0 77.2 reduce-scatter.4
where the time goes:
time: 835 us; the launch traced here: 833 us
  waiting for transfers between devices  551 us (66%)
  local copies, waits for them, and re-layouts  83.3 us (10%)
  other arithmetic  81.7 us (10%)
  blocking collectives  62.1 us (7%)
  matrix products  33.1 us (4%)
  between operations  15.7 us (2%)
    psum x8, waiting for transfers between devices, from_root(): return lax.psum(block, axis)  394 us
    reduce_scatter x1, waiting for transfers between devices, body(): lax.psum_scatter(grad_part, 'narrow', scatter_dimension=0, tiled=True)  78 us
    all_gather x1, waiting for transfers between devices, body(): lax.all_gather(tokens, 'narrow', axis=0, tiled=True)  73.8 us
    psum x8, blocking collectives, from_root(): return lax.psum(block, axis)  62.1 us
    scatter-add x4, other arithmetic, forward(): running.at[:, idx_second]  30.5 us
    scatter-add x4, other arithmetic, backward(): running.at[:, idx_first]  30.5 us
    dynamic_update_slice x24, local copies, waits for them, and re-layouts, receive(): lax.dynamic_update_index_in_dim(buffer, piece[0], section_num, 0)  22.7 us
  transfers between devices with their start and end apart: 12, of which 11 were waited for; matrix products, arithmetic and copies ran while one was open for 20% of the time, Pallas kernels for 0%

commit v1 on v0

--- a/solution.py
+++ b/solution.py
@@ -6,7 +6,10 @@
 
 def from_root(block, axis, source):
     block = jnp.where(lax.axis_index(axis) == source, block, jnp.zeros_like(block))
-    return lax.psum(block, axis)
+    bring_the_pools = lambda inputs, mesh_dim: jnp.sum(
+        lax.all_gather(inputs, axis_name=mesh_dim), axis=0
+    )
+    return bring_the_pools(block, axis)
 
 
 def activate(values):

time: 835 us -> 773 us (0.926)
  waiting for transfers between devices: 551 us -> 374 us
  blocking collectives: 62.1 us -> 133 us
  other arithmetic: 81.7 us -> 129 us
    psum x8 -> x0, waiting for transfers between devices: 394 us -> none  [from_root(): return lax.psum(block, axis)]
    all_gather x0 -> x8, waiting for transfers between devices: none -> 216 us  [from_root(): lax.all_gather(inputs, axis_name=mesh_dim)]
    all_gather x0 -> x8, blocking collectives: none -> 69.4 us  [from_root(): lax.all_gather(inputs, axis_name=mesh_dim)]
    while x0 -> x8, blocking collectives: none -> 63.8 us
    psum x8 -> x0, blocking collectives: 62.1 us -> none  [from_root(): return lax.psum(block, axis)]
    reduce_sum x0 -> x24, other arithmetic: none -> 36.1 us  [from_root(): jnp.sum(lax.all_gather(inputs, axis_name=mesh_dim), axis=0)]
    while x0 -> x16, other arithmetic: none -> 11.6 us
    while x0 -> x16, local copies, waits for them, and re-layouts: none -> 10.5 us
  transfers between devices with their start and end apart: 12 -> 12, of which waited for: 11 -> 11; matrix products, arithmetic and copies ran while one was open for 20% -> 26% of each run, Pallas kernels for 0% -> 0%
where the time goes in v1:
time: 773 us; the launch traced here: 770 us
  waiting for transfers between devices  374 us (48%)
  blocking collectives  133 us (17%)
  other arithmetic  129 us (17%)
  local copies, waits for them, and re-layouts  84.8 us (11%)
  matrix products  33.2 us (4%)
  between operations  15.7 us (2%)
    all_gather x8, waiting for transfers between devices, from_root(): lax.all_gather(inputs, axis_name=mesh_dim)  216 us
    reduce_scatter x1, waiting for transfers between devices, body(): lax.psum_scatter(grad_part, 'narrow', scatter_dimension=0, tiled=True)  77.9 us
    all_gather x1, waiting for transfers between devices, body(): lax.all_gather(tokens, 'narrow', axis=0, tiled=True)  74.6 us
    all_gather x8, blocking collectives, from_root(): lax.all_gather(inputs, axis_name=mesh_dim)  69.4 us
    while x8, blocking collectives  63.8 us
    reduce_sum x24, other arithmetic, from_root(): jnp.sum(lax.all_gather(inputs, axis_name=mesh_dim), axis=0)  36.1 us
    scatter-add x4, other arithmetic, forward(): running.at[:, idx_second]  30.8 us
    scatter-add x4, other arithmetic, backward(): running.at[:, idx_first]  30.5 us
  transfers between devices with their start and end apart: 12, of which 11 were waited for; matrix products, arithmetic and copies ran while one was open for 26% of the time, Pallas kernels for 0%

profile of v1, /device:TPU:0, one launch (start us, length us, event | category | flops | bytes accessed | tf_op | source)
XLA Modules:
  0.0 770.2 jit_solution(9058113078050698652)
XLA Ops:
  10.3 430.7 %while.43 = (s32[]{:T(128)}, bf16[8,6,256,256]{3,2,1,0:T(8,128)(2,1)}, s32[8,6]{1,0:T(8,128)S(1)}, s32[8]{0:T(128)S(1)}, bf16[1,6,256,256]{3,2,1,0:T(8,128)(2,1)...) while((s32[]{:T(128)}, ...), condition=%wide.region_4.5_spmd, body=%wide.region_0.4_spmd.sunk | while | flops 3145800 | bytes 31458272 | solution.py:44
  23.4 8.1 %all-gather.7 = s32[8,1,6]{2,1,0:T(1,128)S(1)} all-gather(s32[1,1,6]{2,1,0:T(1,128)S(1)} %fusion.101), channel_id=3, replica_groups=mesh['wide'=8,'narrow'=4] {'wide'}, dimensions={0}, use_global_device_ids=true | all-gather | bytes 216 | tf_op jit(solution)/shard_map/while/body/eval_jaxpr/all_gather | solution.py:10
  33.0 28.9 %all-gather.16.cloned.1.call-done = bf16[8,6,256,256]{3,2,1,0:T(8,128)(2,1)} async-done(((bf16[1,6,256,256]{3,2,1,0:T(8,128)(2,1)}), bf16[8,6,256,256]{3,2,1,0:T(8,128)(2,1)}) %all-gather.16.cloned.1.call-update) | async-done | bytes 6291472 | tf_op jit(solution)/shard_map/while/body/eval_jaxpr/all_gather | solution.py:10
  77.3 8.7 %all-gather.7 = s32[8,1,6]{2,1,0:T(1,128)S(1)} all-gather(s32[1,1,6]{2,1,0:T(1,128)S(1)} %fusion.101), channel_id=3, replica_groups=mesh['wide'=8,'narrow'=4] {'wide'}, dimensions={0}, use_global_device_ids=true | all-gather | bytes 216 | tf_op jit(solution)/shard_map/while/body/eval_jaxpr/all_gather | solution.py:10
  87.5 27.9 %all-gather.16.cloned.1.call-done = bf16[8,6,256,256]{3,2,1,0:T(8,128)(2,1)} async-done(((bf16[1,6,256,256]{3,2,1,0:T(8,128)(2,1)}), bf16[8,6,256,256]{3,2,1,0:T(8,128)(2,1)}) %all-gather.16.cloned.1.call-update) | async-done | bytes 6291472 | tf_op jit(solution)/shard_map/while/body/eval_jaxpr/all_gather | solution.py:10
  123.8 8.0 %all-reduce.2 = s32[8]{0:T(128)S(1)} all-reduce(s32[8]{0:T(128)S(1)} %select_dynamic-update-slice_fusion.2), channel_id=4, replica_groups=mesh['wide'=8,'narrow'=4] {'wide'}, use_global_device_ids=true, to_apply=%add | all-reduce | flops 8 | bytes 64 | tf_op jit(solution)/shard_map/while
  131.8 9.5 %all-gather.7 = s32[8,1,6]{2,1,0:T(1,128)S(1)} all-gather(s32[1,1,6]{2,1,0:T(1,128)S(1)} %fusion.101), channel_id=3, replica_groups=mesh['wide'=8,'narrow'=4] {'wide'}, dimensions={0}, use_global_device_ids=true | all-gather | bytes 216 | tf_op jit(solution)/shard_map/while/body/eval_jaxpr/all_gather | solution.py:10
  142.8 26.2 %all-gather.16.cloned.1.call-done = bf16[8,6,256,256]{3,2,1,0:T(8,128)(2,1)} async-done(((bf16[1,6,256,256]{3,2,1,0:T(8,128)(2,1)}), bf16[8,6,256,256]{3,2,1,0:T(8,128)(2,1)}) %all-gather.16.cloned.1.call-update) | async-done | bytes 6291472 | tf_op jit(solution)/shard_map/while/body/eval_jaxpr/all_gather | solution.py:10
  185.3 9.5 %all-gather.7 = s32[8,1,6]{2,1,0:T(1,128)S(1)} all-gather(s32[1,1,6]{2,1,0:T(1,128)S(1)} %fusion.101), channel_id=3, replica_groups=mesh['wide'=8,'narrow'=4] {'wide'}, dimensions={0}, use_global_device_ids=true | all-gather | bytes 216 | tf_op jit(solution)/shard_map/while/body/eval_jaxpr/all_gather | solution.py:10
  196.3 26.1 %all-gather.16.cloned.1.call-done = bf16[8,6,256,256]{3,2,1,0:T(8,128)(2,1)} async-done(((bf16[1,6,256,256]{3,2,1,0:T(8,128)(2,1)}), bf16[8,6,256,256]{3,2,1,0:T(8,128)(2,1)}) %all-gather.16.cloned.1.call-update) | async-done | bytes 6291472 | tf_op jit(solution)/shard_map/while/body/eval_jaxpr/all_gather | solution.py:10
  230.9 8.9 %all-reduce.2 = s32[8]{0:T(128)S(1)} all-reduce(s32[8]{0:T(128)S(1)} %select_dynamic-update-slice_fusion.2), channel_id=4, replica_groups=mesh['wide'=8,'narrow'=4] {'wide'}, use_global_device_ids=true, to_apply=%add | all-reduce | flops 8 | bytes 64 | tf_op jit(solution)/shard_map/while
  239.7 8.4 %all-gather.7 = s32[8,1,6]{2,1,0:T(1,128)S(1)} all-gather(s32[1,1,6]{2,1,0:T(1,128)S(1)} %fusion.101), channel_id=3, replica_groups=mesh['wide'=8,'narrow'=4] {'wide'}, dimensions={0}, use_global_device_ids=true | all-gather | bytes 216 | tf_op jit(solution)/shard_map/while/body/eval_jaxpr/all_gather | solution.py:10
  249.6 26.1 %all-gather.16.cloned.1.call-done = bf16[8,6,256,256]{3,2,1,0:T(8,128)(2,1)} async-done(((bf16[1,6,256,256]{3,2,1,0:T(8,128)(2,1)}), bf16[8,6,256,256]{3,2,1,0:T(8,128)(2,1)}) %all-gather.16.cloned.1.call-update) | async-done | bytes 6291472 | tf_op jit(solution)/shard_map/while/body/eval_jaxpr/all_gather | solution.py:10
  291.3 9.9 %all-gather.7 = s32[8,1,6]{2,1,0:T(1,128)S(1)} all-gather(s32[1,1,6]{2,1,0:T(1,128)S(1)} %fusion.101), channel_id=3, replica_groups=mesh['wide'=8,'narrow'=4] {'wide'}, dimensions={0}, use_global_device_ids=true | all-gather | bytes 216 | tf_op jit(solution)/shard_map/while/body/eval_jaxpr/all_gather | solution.py:10
  302.7 26.4 %all-gather.16.cloned.1.call-done = bf16[8,6,256,256]{3,2,1,0:T(8,128)(2,1)} async-done(((bf16[1,6,256,256]{3,2,1,0:T(8,128)(2,1)}), bf16[8,6,256,256]{3,2,1,0:T(8,128)(2,1)}) %all-gather.16.cloned.1.call-update) | async-done | bytes 6291472 | tf_op jit(solution)/shard_map/while/body/eval_jaxpr/all_gather | solution.py:10
  337.5 8.8 %all-reduce.2 = s32[8]{0:T(128)S(1)} all-reduce(s32[8]{0:T(128)S(1)} %select_dynamic-update-slice_fusion.2), channel_id=4, replica_groups=mesh['wide'=8,'narrow'=4] {'wide'}, use_global_device_ids=true, to_apply=%add | all-reduce | flops 8 | bytes 64 | tf_op jit(solution)/shard_map/while
  346.3 8.1 %all-gather.7 = s32[8,1,6]{2,1,0:T(1,128)S(1)} all-gather(s32[1,1,6]{2,1,0:T(1,128)S(1)} %fusion.101), channel_id=3, replica_groups=mesh['wide'=8,'narrow'=4] {'wide'}, dimensions={0}, use_global_device_ids=true | all-gather | bytes 216 | tf_op jit(solution)/shard_map/while/body/eval_jaxpr/all_gather | solution.py:10
  355.8 26.8 %all-gather.16.cloned.1.call-done = bf16[8,6,256,256]{3,2,1,0:T(8,128)(2,1)} async-done(((bf16[1,6,256,256]{3,2,1,0:T(8,128)(2,1)}), bf16[8,6,256,256]{3,2,1,0:T(8,128)(2,1)}) %all-gather.16.cloned.1.call-update) | async-done | bytes 6291472 | tf_op jit(solution)/shard_map/while/body/eval_jaxpr/all_gather | solution.py:10
  391.1 8.6 %all-reduce.2 = s32[8]{0:T(128)S(1)} all-reduce(s32[8]{0:T(128)S(1)} %select_dynamic-update-slice_fusion.2), channel_id=4, replica_groups=mesh['wide'=8,'narrow'=4] {'wide'}, use_global_device_ids=true, to_apply=%add | all-reduce | flops 8 | bytes 64 | tf_op jit(solution)/shard_map/while
  408.3 28.0 %all-gather.16.cloned.1.call-done = bf16[8,6,256,256]{3,2,1,0:T(8,128)(2,1)} async-done(((bf16[1,6,256,256]{3,2,1,0:T(8,128)(2,1)}), bf16[8,6,256,256]{3,2,1,0:T(8,128)(2,1)}) %all-gather.16.cloned.1.call-update) | async-done | bytes 6291472 | tf_op jit(solution)/shard_map/while/body/eval_jaxpr/all_gather | solution.py:10
  449.5 74.6 %all-gather.12.cloned.1.call-done = bf16[512,4096]{0,1:T(8,128)(2,1)} async-done(((bf16[128,4096]{0,1:T(8,128)(2,1)}), bf16[512,4096]{0,1:T(8,128)(2,1)}) %all-gather.12.cloned.1.call-update) | async-done | bytes 4194320 | tf_op jit(solution)/shard_map/all_gather | solution.py:21
  534.5 59.7 %while.44 = (s32[]{:T(128)}, f32[512,16,256]{2,0,1:T(8,128)}, f32[4,512,256]{2,1,0:T(8,128)}, s32[4,6]{1,0:T(4,128)S(1)}, s32[4,6]{1,0:T(4,128)S(1)}, /*index=5*...) while((s32[]{:T(128)}, f32[512,16,256]{2,0,1:T(8,128)}, ...), condition=%wide.region_7.9_spmd, body=%wide.region_5.8_spmd.sunk | while | flops 808059968 | bytes 20452644 | solution.py:84
  615.2 63.1 %while.45 = (s32[]{:T(128)}, f32[512,16,256]{2,0,1:T(8,128)}, s32[4,6]{1,0:T(4,128)S(1)}, s32[4,6]{1,0:T(4,128)S(1)}, bf16[512,16,256]{2,0,1:T(8,128)(2,1)}, /*i...) while((s32[]{:T(128)}, f32[512,16,256]{2,0,1:T(8,128)}, ...), condition=%wide.region_11.13_spmd, body=%wide.region_9.12_spmd.sunk | while | flops 809501760 | bytes 19404576 | solution.py:85
  684.7 77.9 %reduce-scatter.5.cloned.1.call-done = bf16[128,4096]{1,0:T(8,128)(2,1)} async-done(((bf16[512,4096]{1,0:T(8,128)(2,1)}), bf16[128,4096]{1,0:T(8,128)(2,1)}) %reduce-scatter.5.cloned.1.call-update) | async-done | bytes 1048592 | tf_op jit(solution)/shard_map/reduce_scatter | solution.py:90
  (191 shorter events, 288.6 us)
Async XLA Ops:
  10.3 431.4 %copy-start = (bf16[128,4096]{1,0:T(8,128)(2,1)S(1)}, bf16[128,4096]{1,0:T(8,128)(2,1)}, u32[]{:S(2)}) copy-start(bf16[128,4096]{1,0:T(8,128)(2,1)} %param.14) | copy-start | bytes 3145732
  10.3 51.5 %all-gather.16.cloned.1.call-start = ((), (), s32[]{:S(2)}) async-start(), calls=%async_computation.6 | async-start | bytes 7077888 | tf_op jit(solution)/shard_map/while/body/eval_jaxpr/all_gather | solution.py:10
  66.6 48.9 %all-gather.16.cloned.1.call-start = ((), (), s32[]{:S(2)}) async-start(), calls=%async_computation.6 | async-start | bytes 7077888 | tf_op jit(solution)/shard_map/while/body/eval_jaxpr/all_gather | solution.py:10
  120.2 48.9 %all-gather.16.cloned.1.call-start = ((), (), s32[]{:S(2)}) async-start(), calls=%async_computation.6 | async-start | bytes 7077888 | tf_op jit(solution)/shard_map/while/body/eval_jaxpr/all_gather | solution.py:10
  173.8 48.5 %all-gather.16.cloned.1.call-start = ((), (), s32[]{:S(2)}) async-start(), calls=%async_computation.6 | async-start | bytes 7077888 | tf_op jit(solution)/shard_map/while/body/eval_jaxpr/all_gather | solution.py:10
  227.2 48.5 %all-gather.16.cloned.1.call-start = ((), (), s32[]{:S(2)}) async-start(), calls=%async_computation.6 | async-start | bytes 7077888 | tf_op jit(solution)/shard_map/while/body/eval_jaxpr/all_gather | solution.py:10
  280.5 48.5 %all-gather.16.cloned.1.call-start = ((), (), s32[]{:S(2)}) async-start(), calls=%async_computation.6 | async-start | bytes 7077888 | tf_op jit(solution)/shard_map/while/body/eval_jaxpr/all_gather | solution.py:10
  333.8 48.9 %all-gather.16.cloned.1.call-start = ((), (), s32[]{:S(2)}) async-start(), calls=%async_computation.6 | async-start | bytes 7077888 | tf_op jit(solution)/shard_map/while/body/eval_jaxpr/all_gather | solution.py:10
  387.4 48.9 %all-gather.16.cloned.1.call-start = ((), (), s32[]{:S(2)}) async-start(), calls=%async_computation.6 | async-start | bytes 7077888 | tf_op jit(solution)/shard_map/while/body/eval_jaxpr/all_gather | solution.py:10
  441.0 83.0 %all-gather.12.cloned.1.call-start = ((), (), s32[]{:S(2)}) async-start(), calls=%async_computation.2 | async-start | bytes 5242880 | tf_op jit(solution)/shard_map/all_gather | solution.py:21
  441.6 163.1 %all-gather.14.cloned.1.call-start = ((), (), s32[]{:S(2)}) async-start(), calls=%async_computation.4 | async-start | bytes 5242880 | tf_op jit(solution)/shard_map/all_gather | solution.py:22
  443.0 241.7 %reduce-scatter.3.cloned.1.call-start = ((), (), s32[]{:S(2)}) async-start(), calls=%async_computation.3 | async-start | bytes 5242880 | tf_op jit(solution)/shard_map/reduce_scatter | solution.py:89
  600.7 161.9 %reduce-scatter.5.cloned.1.call-start = ((), (), s32[]{:S(2)}) async-start(), calls=%async_computation.5 | async-start | bytes 5242880 | tf_op jit(solution)/shard_map/reduce_scatter | solution.py:90
Sparse Core Ops, SparseCore 0:
  13.6 48.2 all-gather.15
  69.9 45.5 all-gather.15
  123.5 45.5 all-gather.15
  176.8 45.5 all-gather.15
  230.2 45.5 all-gather.15
  283.5 45.5 all-gather.15
  337.1 45.5 all-gather.15
  390.7 45.5 all-gather.15
Sparse Core Ops, SparseCore 1:
  443.6 80.4 all-gather.11
  526.1 78.6 all-gather.13
  607.4 74.9 reduce-scatter.2
  685.4 77.2 reduce-scatter.4
